TPU v7x, 32 devices: a whole 2x2x4 slice. The times are simulated.
32 devices in a mesh: shard: 8 (over z, x), tensor: 4 (over y, core).
Axes of the slice: x: 2, y: 2, z: 4, core: 2. Of those that a mesh axis runs over, the one named last changes fastest.
Arguments:
- mixer_gradient: float32 [3, 1536, 6144], P(None, 'shard', 'tensor'), may hold values from -60 to 60
- output_gradient: float32 [3, 1536, 3072], P(None, 'shard', 'tensor'), may hold values from -60 to 60
- mixer_basis: float32 [3, 1536, 256], P(None, 'shard'), may hold values from -0.21875 to 0.21875
- output_basis: float32 [3, 1536, 256], P(None, 'shard'), may hold values from -0.21875 to 0.21875
- mixer_mean: float32 [256, 3, 6144], P('shard', None, 'tensor'), may hold values from -4 to 4
- mixer_square: float32 [256, 3, 6144], P('shard', None, 'tensor'), may hold values from 0.05 to 2
- output_mean: float32 [256, 3, 3072], P('shard', None, 'tensor'), may hold values from -4 to 4
- output_square: float32 [256, 3, 3072], P('shard', None, 'tensor'), may hold values from 0.05 to 2
Outputs:
- mixer_update: float32 [3, 1536, 6144], P(None, 'shard', 'tensor')
- output_update: float32 [3, 1536, 3072], P(None, 'shard', 'tensor')
- mixer_moment: float32 [256, 3, 6144], P('shard', None, 'tensor')
- mixer_variance: float32 [256, 3, 6144], P('shard', None, 'tensor')
- output_moment: float32 [256, 3, 3072], P('shard', None, 'tensor')
- output_variance: float32 [256, 3, 3072], P('shard', None, 'tensor')
- mixer_refreshed: float32 [3, 1536, 256], P(None, 'shard')
- output_refreshed: float32 [3, 1536, 256], P(None, 'shard')
All inputs are finite; a program needn't handle non-finite values.
Results may differ from a plain program's by a relative error of at most 0.0003.
Values sent between devices are 32-bit elements; how exact they have to be, the bound alone decides.
A program may use at most 128 MiB of HBM per device.

v0:
```python
import jax
import jax.numpy as jnp
from jax import lax
from jax.sharding import PartitionSpec as P

SWEEPS = 3
ADAM_STEP = 10


highest = lax.Precision.HIGHEST
coeff_linear = 3.4445
coeff_square = -4.775
coeff_fourth = 2.0315
scale_epsilon = 1e-06
adam_epsilon = 1e-08
beta_first = 0.9
beta_second = 0.99


def adam_direction(mean, square, projected):
    moment = beta_first * mean + (1.0 - beta_first) * projected
    variance = beta_second * square + (1.0 - beta_second) * projected * projected
    corrected = moment / (1.0 - beta_first**ADAM_STEP)
    spread = jnp.sqrt(variance / (1.0 - beta_second**ADAM_STEP)) + adam_epsilon
    return (moment, variance, corrected / spread)


def adapt_matrix(gradient, basis, mean, square):
    columns = basis
    projected = lax.psum_scatter(
        jnp.einsum("ldr,ldn->rln", columns, gradient, precision=highest),
        "shard",
        scatter_dimension=0,
        tiled=True,
    )
    moment, variance, direction = adam_direction(mean, square, projected)
    power = jnp.einsum(
        "ldn,rln->ldr",
        gradient,
        lax.all_gather(projected, "shard", axis=0, tiled=True),
        precision=highest,
    )
    columns = basis
    update = jnp.einsum(
        "ldr,rln->ldn",
        columns,
        lax.all_gather(direction, "shard", axis=0, tiled=True),
        precision=highest,
    )
    return (update, moment, variance, power)


def gram_of(current):
    return jnp.einsum("ldr,lds->lrs", current, current, precision=highest)


def poly_of(gram):
    squared = jnp.einsum("lrs,lst->lrt", gram, gram, precision=highest)
    return coeff_square * gram + coeff_fourth * squared


def polish(current, gram):
    return coeff_linear * current + jnp.einsum(
        "ldr,lrs->lds", current, poly_of(gram), precision=highest
    )


def orthogonalize(first_power, second_power):
    first_total, second_total = lax.psum(
        (
            jnp.sum(first_power * first_power, axis=(1, 2)),
            jnp.sum(second_power * second_power, axis=(1, 2)),
        ),
        "shard",
    )
    first_current = first_power / (jnp.sqrt(first_total) + scale_epsilon)[:, None, None]
    second_current = second_power / (jnp.sqrt(second_total) + scale_epsilon)[:, None, None]
    for iteration in range(SWEEPS):
        grams = lax.psum((gram_of(first_current), gram_of(second_current)), "shard")
        first_current = polish(first_current, grams[0])
        second_current = polish(second_current, grams[1])
    return (first_current, second_current)


def local(
    mixer_gradient,
    output_gradient,
    mixer_basis,
    output_basis,
    mixer_mean,
    mixer_square,
    output_mean,
    output_square,
):
    mixer_update, mixer_moment, mixer_variance, mixer_partial = adapt_matrix(
        mixer_gradient, mixer_basis, mixer_mean, mixer_square
    )
    output_update, output_moment, output_variance, output_partial = adapt_matrix(
        output_gradient, output_basis, output_mean, output_square
    )
    mixer_power, output_power = lax.psum((mixer_partial, output_partial), "tensor")
    mixer_refreshed, output_refreshed = orthogonalize(mixer_power, output_power)
    return (
        mixer_update,
        output_update,
        mixer_moment,
        mixer_variance,
        output_moment,
        output_variance,
        mixer_refreshed,
        output_refreshed,
    )


def solution(mesh):
    in_specs = (
        P(None, "shard", "tensor"),
        P(None, "shard", "tensor"),
        P(None, "shard", None),
        P(None, "shard", None),
        P("shard", None, "tensor"),
        P("shard", None, "tensor"),
        P("shard", None, "tensor"),
        P("shard", None, "tensor"),
    )
    out_specs = (
        P(None, "shard", "tensor"),
        P(None, "shard", "tensor"),
        P("shard", None, "tensor"),
        P("shard", None, "tensor"),
        P("shard", None, "tensor"),
        P("shard", None, "tensor"),
        P(None, "shard", None),
        P(None, "shard", None),
    )
    return jax.shard_map(local, mesh=mesh, in_specs=in_specs, out_specs=out_specs, check_vma=False)
```

profile of v0, /device:TPU:0, one launch (start us, length us, event | category | flops | bytes accessed | tf_op | source)
XLA Modules:
  0.0 977.1 jit_solution(7648789328144779458)
XLA Ops:
  9.2 10.5 %convolution_bitcast_fusion = f32[256,3,1536]{0,2,1:T(8,128)} fusion(f32[3,192,1536]{2,1,0:T(8,128)S(1)} %copy-done, f32[3,192,256]{2,1,0:T(8,128)} %param.10), kind=kOutput, calls=%fused_computation | convolution fusion | flops 2717908992 | bytes 8847360 | tf_op jit(solution)/shard_map/ldr,ldn->rln/dot_general | solution.py:31
  19.6 7.4 copy.42
  27.1 7.0 convolution_bitcast_fusion.2
  34.1 4.5 copy.46
  40.4 299.9 %all-reduce.20.cloned.1.call-done = (f32[256,3,1536]{2,1,0:T(4,128)}, f32[256,3,768]{2,1,0:T(4,128)}) async-done(((f32[256,3,1536]{2,1,0:T(4,128)}, f32[256,3,768]{2,1,0:T(4,128)}), (f32[256,3,1536]{2,1,0:T(4,128)}, f32[256,3,768]{2,1,0:T(4,128)})) %all-reduce.20.cloned.1.call-update) | async-done | bytes 7077904
  344.9 3.0 add_divide_fusion
  348.2 46.5 %all-gather.11.cloned.1.call-done = f32[256,3,768]{2,0,1:T(8,128)} async-done(((f32[32,3,768]{2,0,1:T(8,128)}), f32[256,3,768]{2,0,1:T(8,128)}) %all-gather.11.cloned.1.call-update) | async-done | bytes 2359312 | tf_op jit(solution)/shard_map/all_gather | solution.py:40
  394.7 5.6 convolution_bitcast_fusion.4
  400.3 75.6 %all-gather.9.cloned.1.call-done = f32[256,3,1536]{2,0,1:T(8,128)} async-done(((f32[32,3,1536]{2,0,1:T(8,128)}), f32[256,3,1536]{2,0,1:T(8,128)}) %all-gather.9.cloned.1.call-update) | async-done | bytes 4718608 | tf_op jit(solution)/shard_map/all_gather | solution.py:40
  475.9 7.8 convolution_bitcast_fusion.5
  483.8 35.7 %all-reduce.22.cloned.1.call-done = (f32[3,192,256]{2,1,0:T(8,128)}, f32[3,192,256]{2,1,0:T(8,128)}) async-done(((f32[3,192,256]{2,1,0:T(8,128)}, f32[3,192,256]{2,1,0:T(8,128)}), (f32[3,192,256]{2,1,0:T(8,128)}, f32[3,192,256]{2,1,0:T(8,128)})) %all-reduce.22.cloned.1.call-update) | async-done | bytes 1179664 | tf_op jit(solution)/shard_map/psum | solution.py:101
  521.0 21.3 %all-reduce.2 = (f32[3]{0:T(128)S(1)}, f32[3]{0:T(128)S(1)}) all-reduce(f32[3]{0:T(128)S(1)} %get-tuple-element.45, f32[3]{0:T(128)S(1)} %get-tuple-element.44), channel_id=1, replica_groups=mesh['shard'=8,'tensor'=4] {'shard'}, use_global_device_ids=true, to_apply=%region_4.0 | all-reduce | flops 6 | bytes 48 | tf_op jit(solution)/shard_map/psum | solution.py:69
  542.3 3.7 fusion.9
  546.0 3.7 fusion.8
  549.7 85.8 %all-reduce.18.cloned.1.call-done = (f32[3,256,256]{2,1,0:T(8,128)}, f32[3,256,256]{2,1,0:T(8,128)}) async-done(((f32[3,256,256]{2,1,0:T(8,128)}, f32[3,256,256]{2,1,0:T(8,128)}), (f32[3,256,256]{2,1,0:T(8,128)}, f32[3,256,256]{2,1,0:T(8,128)})) %all-reduce.18.cloned.1.call-update) | async-done | bytes 1572880 | tf_op jit(solution)/shard_map/psum | solution.py:79
  635.6 2.8 fusion.2
  648.7 87.1 %all-reduce.16.cloned.1.call-done = (f32[3,256,256]{2,1,0:T(8,128)}, f32[3,256,256]{2,1,0:T(8,128)}) async-done(((f32[3,256,256]{2,1,0:T(8,128)}, f32[3,256,256]{2,1,0:T(8,128)}), (f32[3,256,256]{2,1,0:T(8,128)}, f32[3,256,256]{2,1,0:T(8,128)})) %all-reduce.16.cloned.1.call-update) | async-done | bytes 1572880 | tf_op jit(solution)/shard_map/psum | solution.py:79
  745.9 43.6 %all-gather.7.cloned.1.call-done = f32[256,3,768]{2,0,1:T(8,128)} async-done(((f32[32,3,768]{2,0,1:T(8,128)}), f32[256,3,768]{2,0,1:T(8,128)}) %all-gather.7.cloned.1.call-update) | async-done | bytes 2359312 | tf_op jit(solution)/shard_map/all_gather | solution.py:47
  789.5 4.7 convolution_bitcast_fusion.3
  794.2 76.5 %all-gather.5.cloned.1.call-done = f32[256,3,1536]{2,0,1:T(8,128)} async-done(((f32[32,3,1536]{2,0,1:T(8,128)}), f32[256,3,1536]{2,0,1:T(8,128)}) %all-gather.5.cloned.1.call-update) | async-done | bytes 4718608 | tf_op jit(solution)/shard_map/all_gather | solution.py:47
  870.7 7.7 convolution_bitcast_fusion.1
  878.4 83.4 %all-reduce.14.cloned.1.call-done = (f32[3,256,256]{2,1,0:T(8,128)}, f32[3,256,256]{2,1,0:T(8,128)}) async-done(((f32[3,256,256]{2,1,0:T(8,128)}, f32[3,256,256]{2,1,0:T(8,128)}), (f32[3,256,256]{2,1,0:T(8,128)}, f32[3,256,256]{2,1,0:T(8,128)})) %all-reduce.14.cloned.1.call-update) | async-done | bytes 1572880 | tf_op jit(solution)/shard_map/psum | solution.py:79
  961.8 2.9 fusion
  964.8 2.9 convolution_add_fusion
  (62 shorter events, 32.3 us)
Async XLA Ops:
  7.2 2.0 copy-start
  7.2 333.2 %all-reduce.20.cloned.1.call-start = ((), (), s32[]{:S(2)}) async-start(), calls=%async_computation.7 | async-start | bytes 18874368
  38.5 0.7 copy-start.11
  38.6 356.1 %all-gather.11.cloned.1.call-start = ((), (), s32[]{:S(2)}) async-start(), calls=%async_computation.3 | async-start | bytes 2654208 | tf_op jit(solution)/shard_map/all_gather | solution.py:40
  343.6 132.3 %all-gather.9.cloned.1.call-start = ((), (), s32[]{:S(2)}) async-start(), calls=%async_computation.2 | async-start | bytes 5308416 | tf_op jit(solution)/shard_map/all_gather | solution.py:40
  347.9 171.6 %all-reduce.22.cloned.1.call-start = ((), (), s32[]{:S(2)}) async-start(), calls=%async_computation.8 | async-start | bytes 2359296 | tf_op jit(solution)/shard_map/psum | solution.py:101
  483.7 151.8 %all-reduce.18.cloned.1.call-start = ((), (), s32[]{:S(2)}) async-start(), calls=%async_computation.6 | async-start | bytes 3145728 | tf_op jit(solution)/shard_map/psum | solution.py:79
  549.7 186.1 %all-reduce.16.cloned.1.call-start = ((), (), s32[]{:S(2)}) async-start(), calls=%async_computation.5 | async-start | bytes 3145728 | tf_op jit(solution)/shard_map/psum | solution.py:79
  638.4 4.5 copy-start.7
  638.4 5.4 copy-start.10
  647.0 142.5 %all-gather.7.cloned.1.call-start = ((), (), s32[]{:S(2)}) async-start(), calls=%async_computation.1 | async-start | bytes 2654208 | tf_op jit(solution)/shard_map/all_gather | solution.py:47
  647.7 223.0 %all-gather.5.cloned.1.call-start = ((), (), s32[]{:S(2)}) async-start(), calls=%async_computation | async-start | bytes 5308416 | tf_op jit(solution)/shard_map/all_gather | solution.py:47
  648.5 313.4 %all-reduce.14.cloned.1.call-start = ((), (), s32[]{:S(2)}) async-start(), calls=%async_computation.4 | async-start | bytes 3145728 | tf_op jit(solution)/shard_map/psum | solution.py:79
  735.8 5.9 copy-start.5
  739.4 6.5 copy-start.2
  742.7 46.8 %copy-start.8 = (f32[3,192,256]{2,1,0:T(8,128)S(1)}, f32[3,192,256]{2,1,0:T(8,128)}, u32[]{:S(2)}) copy-start(f32[3,192,256]{2,1,0:T(8,128)} %param.11) | copy-start | bytes 1769476
  743.5 50.8 %copy-start.3 = (f32[3,192,256]{2,1,0:T(8,128)}, f32[3,192,256]{2,1,0:T(8,128)S(1)}, u32[]{:S(2)}) copy-start(f32[3,192,256]{2,1,0:T(8,128)S(1)} %convolution_add_fusion.4) | copy-start | bytes 1769476
  745.8 124.9 %copy-start.9 = (f32[3,192,256]{2,1,0:T(8,128)S(1)}, f32[3,192,256]{2,1,0:T(8,128)}, u32[]{:S(2)}) copy-start(f32[3,192,256]{2,1,0:T(8,128)} %param.10) | copy-start | bytes 1769476
  961.8 5.8 copy-start.6
  961.8 6.7 copy-start.4
  961.8 8.3 copy-start.1
Sparse Core Ops, SparseCore 0:
  38.7 301.5 all-reduce.19
  343.7 50.9 all-gather.10
  397.5 78.4 all-gather.8
  483.9 35.6 all-reduce.21
  549.8 85.7 all-reduce.17
  647.1 88.6 all-reduce.15
  738.0 51.4 all-gather.6
  792.3 78.4 all-gather.4
  874.3 87.4 all-reduce.13
where the time goes:
time: 985 us; the launch traced here: 977 us
  waiting for transfers between devices  836 us (85%)
  matrix products  80.2 us (8%)
  blocking collectives  21.3 us (2%)
  local copies, waits for them, and re-layouts  17.4 us (2%)
  between operations  15.1 us (2%)
    unnamed x10, waiting for transfers between devices  301 us
    psum x3, waiting for transfers between devices, orthogonalize(): grams = lax.psum((gram_of(first_current), gram_of(second_current)), 'shard')  256 us
    all_gather x2, waiting for transfers between devices, adapt_matrix(): lax.all_gather(projected, 'shard', axis=0, tiled=True)  122 us
    all_gather x2, waiting for transfers between devices, adapt_matrix(): lax.all_gather(direction, 'shard', axis=0, tiled=True)  120 us
    psum x1, waiting for transfers between devices, local(): lax.psum((mixer_partial, output_partial), 'tensor')  35.7 us
    psum x1, blocking collectives, orthogonalize(): lax.psum((jnp.sum(first_power * first_power, axis=(1, 2)), jnp.sum(second...  21.3 us
  transfers between devices with their start and end apart: 9, of which 9 were waited for; matrix products, arithmetic and copies ran while one was open for 3% of the time, Pallas kernels for 0%

commit v1 on v0

v1 whole, which is shorter than its diff:
```python
import functools

import jax
import jax.numpy as jnp
from jax import lax
from jax.experimental import pallas as pl
from jax.experimental.pallas import tpu as pltpu
from jax.sharding import PartitionSpec as P

SWEEPS = 3
ADAM_STEP = 10

high = lax.Precision.HIGH
highest = lax.Precision.HIGHEST
coeff_linear = 3.4445
coeff_square = -4.775
coeff_fourth = 2.0315
scale_epsilon = 1e-06
adam_epsilon = 1e-08
beta_first = 0.9
beta_second = 0.99

MESH = pl.DeviceIdType.MESH
VMEM_LIMIT = 56 * 2**20


def adam_direction(mean, square, projected):
    moment = beta_first * mean + (1.0 - beta_first) * projected
    variance = beta_second * square + (1.0 - beta_second) * projected * projected
    corrected = moment / (1.0 - beta_first**ADAM_STEP)
    spread = jnp.sqrt(variance / (1.0 - beta_second**ADAM_STEP)) + adam_epsilon
    return (moment, variance, corrected / spread)


def remote(src, dst, send, recv, device):
    return pltpu.make_async_remote_copy(
        src_ref=src,
        dst_ref=dst,
        send_sem=send,
        recv_sem=recv,
        device_id=device,
        device_id_type=MESH,
    )


def place(groups):
    me = lax.axis_index("shard")
    return me // 2, lax.rem(me, 2)


def peer(line, side, step, groups):
    other = lax.rem(line + step, groups)
    return other, {"shard": other * 2 + side}


def greet(groups, tensor_peers=()):
    line, side = place(groups)
    barrier = pltpu.get_barrier_semaphore()
    devices = [peer(line, side, step, groups)[1] for step in range(1, groups)]
    devices.append({"shard": line * 2 + 1 - side})
    devices.extend({"tensor": other} for other in tensor_peers)
    for device in devices:
        pl.semaphore_signal(barrier, inc=1, device_id=device, device_id_type=MESH)
    pl.semaphore_wait(barrier, len(devices))


def units_of(refs):
    return [(which, layer) for layer in range(refs[0].shape[0]) for which in range(len(refs))]


def gather_one(groups, u, m, l, own, full, sems):
    line, side = place(groups)
    zs, zr, xs, xr = sems
    copies = []
    for step in range(1, groups):
        _, device = peer(line, side, step, groups)
        copy = remote(
            own[m].at[l], full[m].at[l, line, side], zs.at[u, step], zr.at[u, step], device
        )
        copy.start()
        copies.append(copy)
    pair = remote(
        own[m].at[l],
        full[m].at[l, line, side],
        xs.at[u, 0],
        xr.at[u, 0],
        {"shard": line * 2 + 1 - side},
    )
    pair.start()
    full[m][l, line, side] = own[m][l]
    return copies + [pair]


def gather_forward(groups, u, m, l, full, sems):
    line, side = place(groups)
    zs, zr, xs, xr = sems
    forwards = []
    for step in range(1, groups):
        source = lax.rem(line + groups - step, groups)
        block = full[m].at[l, source, side]
        landed = remote(
            block, block, zs.at[u, step], zr.at[u, step], {"shard": line * 2 + 1 - side}
        )
        landed.wait_recv()
        forward = remote(
            block, block, xs.at[u, step], xr.at[u, step], {"shard": line * 2 + 1 - side}
        )
        forward.start()
        forwards.append(forward)
    return forwards


def gather_finish(groups, u, m, l, full, sems, sent, forwards):
    line, side = place(groups)
    zs, zr, xs, xr = sems
    for copy in sent:
        copy.wait_send()
    for copy in forwards:
        copy.wait_send()
    for step in range(groups):
        source = lax.rem(line + groups - step, groups)
        block = full[m].at[l, source, 1 - side]
        remote(
            block, block, xs.at[u, step], xr.at[u, step], {"shard": line * 2 + 1 - side}
        ).wait_recv()


def scatter_pair(u, m, l, parts, pair_buf, sems, groups):
    line, side = place(groups)
    copy = remote(
        parts[m].at[l, :, 1 - side],
        pair_buf[m].at[l],
        sems[0].at[u],
        sems[1].at[u],
        {"shard": line * 2 + 1 - side},
    )
    copy.start()
    return copy


def scatter_line(u, m, l, parts, pair_buf, line_buf, copy, sems, groups):
    line, side = place(groups)
    copy.wait_recv()
    for g in range(groups):
        pair_buf[m][l, g] = pair_buf[m][l, g] + parts[m][l, g, side]
    sent = []
    for step in range(1, groups):
        other, device = peer(line, side, step, groups)
        out = remote(
            pair_buf[m].at[l, other],
            line_buf[m].at[l, step - 1],
            sems[2].at[u, step],
            sems[3].at[u, step],
            device,
        )
        out.start()
        sent.append(out)
    return sent


def scatter_sum(m, l, pair_buf, line_buf, sent, groups):
    line, _ = place(groups)
    total = pair_buf[m][l, line]
    for step in range(1, groups):
        sent[step - 1].wait_recv()
        total = total + line_buf[m][l, step - 1]
    return total


def reduce_kernel(groups, count, adam, *refs):
    parts = refs[:count]
    refs = refs[count:]
    if adam:
        means, squares = refs[:count], refs[count : 2 * count]
        refs = refs[2 * count :]
    full = refs[:count]
    refs = refs[count:]
    if adam:
        moments, variances, directions = (
            refs[:count],
            refs[count : 2 * count],
            refs[2 * count : 3 * count],
        )
        refs = refs[3 * count :]
    own, pair_buf, line_buf = (
        refs[:count],
        refs[count : 2 * count],
        refs[2 * count : 3 * count],
    )
    sems = refs[3 * count :]
    scatter_sems, gather_sems = sems[:4], sems[4:]
    greet(groups)
    units = units_of(parts)
    pairs = [scatter_pair(u, m, l, parts, pair_buf, scatter_sems, groups) for u, (m, l) in enumerate(units)]
    lines, sent, forwards = {}, {}, {}
    lag_sum, lag_forward = 1, 3
    for tick in range(len(units) + lag_forward):
        if tick < len(units):
            m, l = units[tick]
            lines[tick] = scatter_line(
                tick, m, l, parts, pair_buf, line_buf, pairs[tick], scatter_sems, groups
            )
        u = tick - lag_sum
        if 0 <= u < len(units):
            m, l = units[u]
            own[m][l] = scatter_sum(m, l, pair_buf, line_buf, lines[u], groups)
            sent[u] = gather_one(groups, u, m, l, own, full, gather_sems)
            if adam:
                moment, variance, direction = adam_direction(means[m][l], squares[m][l], own[m][l])
                moments[m][l] = moment
                variances[m][l] = variance
                directions[m][l] = direction
        u = tick - lag_forward
        if 0 <= u < len(units):
            m, l = units[u]
            forwards[u] = gather_forward(groups, u, m, l, full, gather_sems)
    for u, (m, l) in enumerate(units):
        gather_finish(groups, u, m, l, full, gather_sems, sent[u], forwards[u])
        pairs[u].wait_send()
        for copy in lines[u]:
            copy.wait_send()


def gather_sem_shapes(units, groups):
    return [pltpu.SemaphoreType.DMA((units, groups))] * 4


def reduce_call(parts, means, squares, shard, collective):
    groups = shard // 2
    count = len(parts)
    adam = means is not None
    layers, rank, _ = parts[0].shape
    rows = rank // shard
    parts = [p.reshape(layers, groups, 2, rows, p.shape[2]) for p in parts]
    widths = [p.shape[4] for p in parts]
    units = count * layers
    vmem = pl.BlockSpec(memory_space=pltpu.VMEM)
    full = [jax.ShapeDtypeStruct(p.shape, p.dtype) for p in parts]
    small = [jax.ShapeDtypeStruct((layers, rows, w), jnp.float32) for w in widths]
    outs = full + (small * 3 if adam else [])
    args = list(parts) + (list(means) + list(squares) if adam else [])
    result = pl.pallas_call(
        functools.partial(reduce_kernel, groups, count, adam),
        out_shape=outs,
        in_specs=[vmem] * len(args),
        out_specs=[vmem] * len(outs),
        scratch_shapes=[pltpu.VMEM((layers, rows, w), jnp.float32) for w in widths]
        + [pltpu.VMEM((layers, groups, rows, w), jnp.float32) for w in widths]
        + [pltpu.VMEM((layers, groups - 1, rows, w), jnp.float32) for w in widths]
        + [pltpu.SemaphoreType.DMA((units,))] * 2
        + [pltpu.SemaphoreType.DMA((units, groups))] * 2
        + gather_sem_shapes(units, groups),
        compiler_params=pltpu.CompilerParams(
            collective_id=collective, has_side_effects=True, vmem_limit_bytes=VMEM_LIMIT
        ),
        name="reduce_gather_adam" if adam else "reduce_gather",
    )(*args)
    whole = [r.reshape(layers, rank, r.shape[4]) for r in result[:count]]
    return whole, [result[count * k : count * (k + 1)] for k in range(1, 4 if adam else 1)]


def gather_power_kernel(groups, count, *refs):
    own, powers = refs[:count], refs[count : 2 * count]
    refs = refs[2 * count :]
    full, sums = refs[:count], refs[count : 2 * count]
    refs = refs[2 * count :]
    first, half, second = refs[:count], refs[count : 2 * count], refs[2 * count : 3 * count]
    sems = refs[3 * count :]
    gather_sems = sems[:4]
    send, recv = sems[4:]
    me = lax.axis_index("tensor")
    side = lax.rem(me, 2)
    near = me + 1 - 2 * side
    far = lax.rem(me + 2, 4)
    greet(groups, (near, far))
    for_near = [
        remote(powers[m].at[:, 1 - side], first[m], send.at[0, m], recv.at[0, m], {"tensor": near})
        for m in range(count)
    ]
    for copy in for_near:
        copy.start()
    units = units_of(own)
    sent = [gather_one(groups, u, m, l, own, full, gather_sems) for u, (m, l) in enumerate(units)]
    for_far = []
    for m in range(count):
        for_near[m].wait_recv()
        half[m][...] = powers[m][:, side] + first[m][...]
        copy = remote(half[m], second[m], send.at[1, m], recv.at[1, m], {"tensor": far})
        copy.start()
        for_far.append(copy)
    forwards = [gather_forward(groups, u, m, l, full, gather_sems) for u, (m, l) in enumerate(units)]
    back = []
    for m in range(count):
        for_far[m].wait_recv()
        sums[m][:, side] = half[m][...] + second[m][...]
        copy = remote(
            sums[m].at[:, side], sums[m].at[:, side], send.at[2, m], recv.at[2, m], {"tensor": near}
        )
        copy.start()
        back.append(copy)
    for u, (m, l) in enumerate(units):
        gather_finish(groups, u, m, l, full, gather_sems, sent[u], forwards[u])
    for m in range(count):
        for_near[m].wait_send()
        for_far[m].wait_send()
        back[m].wait_send()
        remote(
            sums[m].at[:, 1 - side],
            sums[m].at[:, 1 - side],
            send.at[2, m],
            recv.at[2, m],
            {"tensor": near},
        ).wait_recv()


def gather_power_call(own, powers, shard, collective):
    groups = shard // 2
    count = len(own)
    layers, rows, _ = own[0].shape
    widths = [o.shape[2] for o in own]
    depth, rank = powers[0].shape[1:]
    powers = [p.reshape(layers, 2, depth // 2, rank) for p in powers]
    units = count * layers
    vmem = pl.BlockSpec(memory_space=pltpu.VMEM)
    outs = [
        jax.ShapeDtypeStruct((layers, groups, 2, rows, w), jnp.float32) for w in widths
    ] + [jax.ShapeDtypeStruct(p.shape, jnp.float32) for p in powers]
    halves = [pltpu.VMEM((layers, depth // 2, rank), jnp.float32) for _ in powers]
    result = pl.pallas_call(
        functools.partial(gather_power_kernel, groups, count),
        out_shape=outs,
        in_specs=[vmem] * (2 * count),
        out_specs=[vmem] * len(outs),
        scratch_shapes=halves * 3
        + gather_sem_shapes(units, groups)
        + [pltpu.SemaphoreType.DMA((3, count))] * 2,
        compiler_params=pltpu.CompilerParams(
            collective_id=collective, has_side_effects=True, vmem_limit_bytes=VMEM_LIMIT
        ),
        name="gather_power",
    )(*own, *powers)
    whole = [r.reshape(layers, 2 * groups * rows, r.shape[4]) for r in result[:count]]
    return whole, [r.reshape(layers, depth, rank) for r in result[count:]]


def mix(left, right):
    return jnp.einsum("lrs,lst->lrt", left, right, precision=highest)


def refresh(gram):
    rank = gram.shape[-1]
    eye = jnp.eye(rank, dtype=jnp.float32)
    total = jnp.sum(gram * eye, axis=(1, 2))
    scale = jnp.sqrt(total) + scale_epsilon
    gram = gram / scale[:, None, None] / scale[:, None, None]
    product = None
    for sweep in range(SWEEPS):
        factor = coeff_linear * eye + coeff_square * gram + coeff_fourth * mix(gram, gram)
        product = factor if product is None else mix(product, factor)
        if sweep + 1 < SWEEPS:
            gram = mix(factor, mix(gram, factor))
    return product, scale


def local(shard, *args):
    gradients, bases, moments_in = args[0:2], args[2:4], args[4:8]
    partial = [
        jnp.einsum("ldr,ldn->lrn", basis, gradient, precision=high)
        for gradient, basis in zip(gradients, bases)
    ]
    flipped = [jnp.transpose(a, (1, 0, 2)) for a in moments_in]
    projected, (moment, variance, direction) = reduce_call(
        partial, flipped[0::2], flipped[1::2], shard, 1
    )
    partial_power = [
        jnp.einsum("ldn,lrn->ldr", gradient, rows, precision=high)
        for gradient, rows in zip(gradients, projected)
    ]
    directions, power = gather_power_call(direction, partial_power, shard, 2)
    grams = jnp.concatenate(
        [jnp.einsum("ldr,lds->lrs", p, p, precision=highest) for p in power], axis=2
    )
    (grams,), _ = reduce_call([grams], None, None, shard, 3)
    rank = grams.shape[1]
    layers = grams.shape[0]
    stacked = jnp.concatenate([grams[:, :, :rank], grams[:, :, rank:]], axis=0)
    factors, scale = refresh(stacked)
    updates = [
        jnp.einsum("ldr,lrn->ldn", basis, rows, precision=high)
        for basis, rows in zip(bases, directions)
    ]
    refreshed = [
        jnp.einsum(
            "ldr,lrs->lds",
            p / scale[layers * m : layers * (m + 1), None, None],
            factors[layers * m : layers * (m + 1)],
            precision=highest,
        )
        for m, p in enumerate(power)
    ]
    back = [jnp.transpose(a, (1, 0, 2)) for pair in zip(moment, variance) for a in pair]
    return (*updates, *back, *refreshed)


def solution(mesh):
    wide, low, basis = P(None, "shard", "tensor"), P("shard", None, "tensor"), P(None, "shard", None)
    return jax.shard_map(
        functools.partial(local, mesh.shape["shard"]),
        mesh=mesh,
        in_specs=(wide, wide, basis, basis, low, low, low, low),
        out_specs=(wide, wide, low, low, low, low, basis, basis),
        check_vma=False,
    )
```

time: 985 us -> 401 us (0.41)
  waiting for transfers between devices: 836 us -> 0 us
  Pallas kernels: 0 us -> 341 us
  matrix products: 80.2 us -> 47.5 us
  blocking collectives: 21.3 us -> 0 us
  between operations: 15.1 us -> 0.85 us
    pallas_call x0 -> x3, Pallas kernels: none -> 341 us  [the longest x2 243 us: reduce_call(): pl.pallas_call(functools.partial(reduce_kernel, groups, count, adam), out...]
    unnamed x10 -> x0, waiting for transfers between devices: 301 us -> none
    psum x4 -> x0, waiting for transfers between devices: 292 us -> none  [the longest x3 256 us: orthogonalize(): grams = lax.psum((gram_of(first_current), gram_of(second_current)), 'shard')]
    all_gather x4 -> x0, waiting for transfers between devices: 242 us -> none  [the longest x2 122 us: adapt_matrix(): lax.all_gather(projected, 'shard', axis=0, tiled=True)]
    dot_general x24 -> x19, matrix products: 80.2 us -> 47.5 us  [the longest x9 17 us: mix(): return jnp.einsum('lrs,lst->lrt', left, right, precision=highest)]
    psum x1 -> x0, blocking collectives: 21.3 us -> none  [orthogonalize(): lax.psum((jnp.sum(first_power * first_power, axis=(1, 2)), jnp.sum(second...]
    transpose x2 -> x0, local copies, waits for them, and re-layouts: 11.9 us -> none  [adapt_matrix(): jnp.einsum('ldr,ldn->rln', columns, gradient, precision=highest)]
  transfers between devices with their start and end apart: 9 -> 0, of which waited for: 9 -> 0; matrix products, arithmetic and copies ran while one was open for 3% -> 0% of each run, Pallas kernels for 0% -> 0%
where the time goes in v1:
time: 401 us
  Pallas kernels  341 us (85%)
  matrix products  47.5 us (12%)
  local copies, waits for them, and re-layouts  9.69 us (2%)
    pallas_call x2, Pallas kernels, reduce_call(): pl.pallas_call(functools.partial(reduce_kernel, groups, count, adam), out...  243 us
    pallas_call x1, Pallas kernels, gather_power_call(): pl.pallas_call(functools.partial(gather_power_kernel, groups, count), out...  98.3 us
    dot_general x9, matrix products, mix(): return jnp.einsum('lrs,lst->lrt', left, right, precision=highest)  17 us
    dot_general x2, matrix products, local(): jnp.einsum('ldr,lrn->ldn', basis, rows, precision=high)  8.3 us
    dot_general x2, matrix products, local(): jnp.einsum('ldr,ldn->lrn', basis, gradient, precision=high)  8.11 us

profile of v1, /device:TPU:0, one launch (start us, length us, event | category | flops | bytes accessed | tf_op | source)
XLA Modules:
  0.0 401.0 jit_solution(6109020154051662079)
XLA Ops:
  0.7 2.0 copy-done
  2.6 5.5 %fusion.65 = f32[3,256,1536]{2,1,0:T(8,128)} fusion(f32[3,192,256]{2,1,0:T(8,128)} %param.10, f32[3,192,1536]{2,1,0:T(8,128)S(1)} %copy-done), kind=kOutput, calls=%fused_computation.70 | convolution fusion | flops 1358954496 | bytes 8847360 | tf_op jit(solution)/shard_map/ldr,ldn->lrn/dot_general | solution.py:368
  8.1 2.6 fusion.66
  10.8 193.6 %reduce_gather_adam.1 = (f32[3,4,2,32,1536]{4,3,2,1,0:T(8,128)}, f32[3,4,2,32,768]{4,3,2,1,0:T(8,128)}, f32[3,32,1536]{2,1,0:T(8,128)}, f32[3,32,768]{2,1,0:T(8,...) custom-call(f32[3,4,2,32,1536]{4,3,2,1,0:T(8,128)} %bitcast.52, ...), custom_call_target="tpu_custom_call" | custom-call | tf_op jit(solution)/shard_map/reduce_gather_adam/pallas_call | solution.py:242
  204.4 5.8 %fusion.67 = f32[3,256,192]{1,2,0:T(8,128)} fusion(f32[3,256,1536]{2,1,0:T(8,128)} %bitcast.56, f32[3,192,1536]{2,1,0:T(8,128)S(1)} %copy-done), kind=kOutput, calls=%fused_computation.72 | convolution fusion | flops 1358954496 | bytes 8847360 | tf_op jit(solution)/shard_map/ldn,lrn->ldr/dot_general | solution.py:376
  210.2 2.1 fusion.68
  212.3 98.3 %gather_power.1 = (f32[3,4,2,32,1536]{4,3,2,1,0:T(8,128)}, f32[3,4,2,32,768]{4,3,2,1,0:T(8,128)}, f32[3,2,96,256]{3,2,1,0:T(8,128)}, f32[3,2,96,256]{3,2,1,0:T(8,128)}) custom-call(f32[3,32,1536]{2,1,0:T(8,128)} %get-tuple-element.20.refs_0_, f32[3,32,768]{2,1,0:T(8,128)} %get-tuple-element.21.refs_1_, f32[3,2,96,256]{3,2,1,0:T(8,128)} %bitcast.58, ...), custom_call_target="tpu_custom_call" | custom-call | tf_op jit(solution)/shard_map/gather_power/pallas_call | solution.py:329
  310.6 6.0 %convolution_bitcast_fusion = f32[3,192,1536]{2,1,0:T(8,128)} fusion(f32[3,256,1536]{2,1,0:T(8,128)} %bitcast.57, f32[3,192,256]{2,1,0:T(8,128)S(1)} %copy-done.2), kind=kOutput, calls=%fused_computation | convolution fusion | flops 1358954496 | bytes 8847360 | tf_op jit(solution)/shard_map/ldr,lrn->ldn/dot_general | solution.py:389
  316.6 2.3 convolution_bitcast_fusion.1
  319.0 1.5 fusion.70
  320.5 1.5 fusion.69
  323.2 3.1 copy.16
  326.3 49.5 %reduce_gather.1 = f32[3,4,2,32,512]{4,3,2,1,0:T(8,128)} custom-call(f32[3,4,2,32,512]{4,3,2,1,0:T(8,128)} %bitcast.55), custom_call_target="tpu_custom_call" | custom-call | tf_op jit(solution)/shard_map/reduce_gather/pallas_call | solution.py:242
  377.5 1.8 fusion.60
  379.4 2.0 fusion.12
  381.4 1.9 fusion.11
  383.4 1.9 fusion.71
  385.3 2.1 fusion.7
  387.4 1.8 fusion.6
  389.2 1.9 fusion.5
  391.1 1.7 fusion.72
  392.8 1.9 fusion
  394.7 1.6 fusion.19
  396.3 1.6 fusion.17
  (38 shorter events, 6.2 us)
Async XLA Ops:
  0.6 2.0 copy-start
  0.6 7.5 %copy-start.3 = (f32[3,192,256]{2,1,0:T(8,128)S(1)}, f32[3,192,256]{2,1,0:T(8,128)}, u32[]{:S(2)}) copy-start(f32[3,192,256]{2,1,0:T(8,128)} %param.11) | copy-start | bytes 1769476
  0.7 7.5 %copy-start.1 = (f32[3,192,768]{2,1,0:T(8,128)S(1)}, f32[3,192,768]{2,1,0:T(8,128)}, u32[]{:S(2)}) copy-start(f32[3,192,768]{2,1,0:T(8,128)} %param.9) | copy-start | bytes 5308420
  204.4 5.8 %copy-start.4 = (f32[3,4,2,32,768]{4,3,2,1,0:T(8,128)S(1)}, f32[3,4,2,32,768]{4,3,2,1,0:T(8,128)}, u32[]{:S(2)}) copy-start(f32[3,4,2,32,768]{4,3,2,1,0:T(8,128)} %get-tuple-element.23) | copy-start | bytes 7077892
  212.3 98.3 %copy-start.2 = (f32[3,192,256]{2,1,0:T(8,128)S(1)}, f32[3,192,256]{2,1,0:T(8,128)}, u32[]{:S(2)}) copy-start(f32[3,192,256]{2,1,0:T(8,128)} %param.10) | copy-start | bytes 1769476
  310.6 6.0 %copy-start.5 = (f32[3,4,2,32,768]{4,3,2,1,0:T(8,128)S(1)}, f32[3,4,2,32,768]{4,3,2,1,0:T(8,128)}, u32[]{:S(2)}) copy-start(f32[3,4,2,32,768]{4,3,2,1,0:T(8,128)} %get-tuple-element.25) | copy-start | bytes 7077892
  316.6 2.3 copy-start.6
  318.9 1.5 copy-start.8
  392.8 2.0 copy-start.9
  394.6 1.7 copy-start.7
  396.3 1.6 copy-start.11
  396.3 2.4 copy-start.10
  397.9 1.6 copy-start.13
  397.9 2.4 copy-start.12

commit v2 on v0

v2 whole, which is shorter than its diff:
```python
import functools

import jax
import jax.numpy as jnp
from jax import lax
from jax.experimental import pallas as pl
from jax.experimental.pallas import tpu as pltpu
from jax.sharding import PartitionSpec as P

SWEEPS = 3
ADAM_STEP = 10

high = lax.Precision.HIGH
highest = lax.Precision.HIGHEST
coeff_linear = 3.4445
coeff_square = -4.775
coeff_fourth = 2.0315
scale_epsilon = 1e-06
adam_epsilon = 1e-08
beta_first = 0.9
beta_second = 0.99

MESH = pl.DeviceIdType.MESH
VMEM_LIMIT = 56 * 2**20


def adam_direction(mean, square, projected):
    moment = beta_first * mean + (1.0 - beta_first) * projected
    variance = beta_second * square + (1.0 - beta_second) * projected * projected
    corrected = moment / (1.0 - beta_first**ADAM_STEP)
    spread = jnp.sqrt(variance / (1.0 - beta_second**ADAM_STEP)) + adam_epsilon
    return (moment, variance, corrected / spread)


def remote(src, dst, send, recv, device):
    return pltpu.make_async_remote_copy(
        src_ref=src,
        dst_ref=dst,
        send_sem=send,
        recv_sem=recv,
        device_id=device,
        device_id_type=MESH,
    )


def place():
    me = lax.axis_index("shard")
    return me // 2, lax.rem(me, 2)


def greet(groups, tensor_peers=()):
    line, side = place()
    barrier = pltpu.get_barrier_semaphore()
    devices = [right_of(groups), left_of(groups), pair_of()]
    devices.extend({"tensor": other} for other in tensor_peers)
    for device in devices:
        pl.semaphore_signal(barrier, inc=1, device_id=device, device_id_type=MESH)
    pl.semaphore_wait(barrier, len(devices))


def right_of(groups):
    line, side = place()
    return {"shard": lax.rem(line + 1, groups) * 2 + side}


def left_of(groups):
    line, side = place()
    return {"shard": lax.rem(line + groups - 1, groups) * 2 + side}


def pair_of():
    line, side = place()
    return {"shard": line * 2 + 1 - side}


def units_of(refs):
    return [(which, layer) for layer in range(refs[0].shape[0]) for which in range(len(refs))]


class Gather:
    def __init__(self, groups, own, full, sems):
        self.groups, self.own, self.full, self.sems = groups, own, full, sems
        self.units = units_of(own)
        self.started = []

    def send(self, u):
        m, l = self.units[u]
        line, side = place()
        zs, zr, xs, xr = self.sems
        source, target = self.own[m].at[l], self.full[m].at[l, line, side]
        ahead = remote(source, target, zs.at[u, 1], zr.at[u, 1], right_of(self.groups))
        ahead.start()
        pair = remote(source, target, xs.at[u, 0], xr.at[u, 0], pair_of())
        pair.start()
        self.full[m][l, line, side] = self.own[m][l]
        self.started += [ahead, pair]

    def hop(self, u, step):
        m, l = self.units[u]
        line, side = place()
        zs, zr, xs, xr = self.sems
        block = self.full[m].at[l, lax.rem(line + self.groups - step, self.groups), side]
        remote(block, block, zs.at[u, step], zr.at[u, step], right_of(self.groups)).wait_recv()
        if step + 1 < self.groups:
            ahead = remote(
                block, block, zs.at[u, step + 1], zr.at[u, step + 1], right_of(self.groups)
            )
            ahead.start()
            self.started.append(ahead)
        pair = remote(block, block, xs.at[u, step], xr.at[u, step], pair_of())
        pair.start()
        self.started.append(pair)

    def landed(self, u):
        m, l = self.units[u]
        line, side = place()
        zs, zr, xs, xr = self.sems
        for step in range(self.groups):
            source = lax.rem(line + self.groups - step, self.groups)
            block = self.full[m].at[l, source, 1 - side]
            remote(block, block, xs.at[u, step], xr.at[u, step], pair_of()).wait_recv()

    def drain(self):
        for copy in self.started:
            copy.wait_send()


class Scatter:
    def __init__(self, groups, parts, pair_buf, line_buf, own, sems):
        self.groups, self.parts, self.own, self.sems = groups, parts, own, sems
        self.pair_buf, self.line_buf = pair_buf, line_buf
        self.units = units_of(parts)
        self.started = []
        self.pairs = {}

    def send(self, u):
        m, l = self.units[u]
        line, side = place()
        copy = remote(
            self.parts[m].at[l, :, 1 - side],
            self.pair_buf[m].at[l],
            self.sems[0].at[u],
            self.sems[1].at[u],
            pair_of(),
        )
        copy.start()
        self.pairs[u] = copy
        self.started.append(copy)

    def ahead(self, u, step, block):
        m, l = self.units[u]
        copy = remote(
            block,
            self.line_buf[m].at[l, step - 1],
            self.sems[2].at[u, step],
            self.sems[3].at[u, step],
            right_of(self.groups),
        )
        copy.start()
        self.started.append(copy)

    def pair(self, u):
        m, l = self.units[u]
        line, side = place()
        self.pairs[u].wait_recv()
        held, part = self.pair_buf[m], self.parts[m]
        first = lax.rem(line + self.groups - 1, self.groups)
        held[l, first] = held[l, first] + part[l, first, side]
        self.ahead(u, 1, held.at[l, first])
        for step in range(1, self.groups):
            g = lax.rem(line + 2 * self.groups - 1 - step, self.groups)
            held[l, g] = held[l, g] + part[l, g, side]

    def hop(self, u, step):
        m, l = self.units[u]
        line, side = place()
        buf = self.line_buf[m]
        block = buf.at[l, step - 1]
        remote(
            block, block, self.sems[2].at[u, step], self.sems[3].at[u, step], right_of(self.groups)
        ).wait_recv()
        g = lax.rem(line + 2 * self.groups - 1 - step, self.groups)
        total = buf[l, step - 1] + self.pair_buf[m][l, g]
        if step + 1 < self.groups:
            buf[l, step - 1] = total
            self.ahead(u, step + 1, block)
        else:
            self.own[m][l] = total

    def drain(self):
        for copy in self.started:
            copy.wait_send()


def reduce_events(scatter, gather, sizes, begin, delay, finish=None):
    events = []
    groups = scatter.groups
    clock = begin
    for u in range(len(scatter.units)):
        clock += sizes[u]
        events.append((clock, functools.partial(scatter.pair, u)))
        for step in range(1, groups):
            events.append((clock + delay * step, functools.partial(scatter.hop, u, step)))
        ready = clock + delay * (groups - 1)
        events.append((ready, functools.partial(gather.send, u)))
        if finish is not None:
            events.append((ready, functools.partial(finish, u)))
        for step in range(1, groups):
            events.append((ready + delay * step, functools.partial(gather.hop, u, step)))
    return events


def play(events):
    for _, action in sorted(events, key=lambda event: event[0]):
        action()


def reduce_kernel(groups, count, *refs):
    def take():
        nonlocal refs
        head, refs = refs[:count], refs[count:]
        return head

    parts, means, squares = take(), take(), take()
    full, moments, variances, directions = take(), take(), take(), take()
    own, pair_buf, line_buf = take(), take(), take()
    scatter = Scatter(groups, parts, pair_buf, line_buf, own, refs[:4])
    gather = Gather(groups, own, full, refs[4:])
    greet(groups)
    for u in range(len(scatter.units)):
        scatter.send(u)

    def adam(u):
        m, l = scatter.units[u]
        moment, variance, direction = adam_direction(means[m][l], squares[m][l], own[m][l])
        moments[m][l] = moment
        variances[m][l] = variance
        directions[m][l] = direction

    most = max(p.shape[-1] for p in parts)
    sizes = [16.0 * parts[m].shape[-1] / most for m, _ in scatter.units]
    play(reduce_events(scatter, gather, sizes, 0.0, 6.0, adam))
    for u in range(len(scatter.units)):
        gather.landed(u)
    scatter.drain()
    gather.drain()


def reduce_scratch(layers, groups, rows, widths):
    return (
        [pltpu.VMEM((layers, rows, w), jnp.float32) for w in widths]
        + [pltpu.VMEM((layers, groups, rows, w), jnp.float32) for w in widths]
        + [pltpu.VMEM((layers, groups - 1, rows, w), jnp.float32) for w in widths]
    )


def scatter_sems(units, groups):
    return [pltpu.SemaphoreType.DMA((units,))] * 2 + [pltpu.SemaphoreType.DMA((units, groups))] * 2


def gather_sems(units, groups):
    return [pltpu.SemaphoreType.DMA((units, groups))] * 4


def reduce_call(parts, means, squares, shard, collective):
    groups = shard // 2
    count = len(parts)
    layers, rank, _ = parts[0].shape
    rows = rank // shard
    parts = [p.reshape(layers, groups, 2, rows, p.shape[2]) for p in parts]
    widths = [p.shape[4] for p in parts]
    units = count * layers
    vmem = pl.BlockSpec(memory_space=pltpu.VMEM)
    outs = [jax.ShapeDtypeStruct(p.shape, p.dtype) for p in parts]
    outs += [jax.ShapeDtypeStruct((layers, rows, w), jnp.float32) for w in widths] * 3
    result = pl.pallas_call(
        functools.partial(reduce_kernel, groups, count),
        out_shape=outs,
        in_specs=[vmem] * (3 * count),
        out_specs=[vmem] * len(outs),
        scratch_shapes=reduce_scratch(layers, groups, rows, widths)
        + scatter_sems(units, groups)
        + gather_sems(units, groups),
        compiler_params=pltpu.CompilerParams(
            collective_id=collective, has_side_effects=True, vmem_limit_bytes=VMEM_LIMIT
        ),
        name="reduce_gather_adam",
    )(*parts, *means, *squares)
    whole = [r.reshape(layers, rank, r.shape[4]) for r in result[:count]]
    return whole, [result[count * k : count * (k + 1)] for k in range(1, 4)]


def mix(left, right):
    return jnp.dot(left, right, precision=highest, preferred_element_type=jnp.float32)


def refresh(gram):
    rank = gram.shape[-1]
    eye = (
        lax.broadcasted_iota(jnp.int32, (rank, rank), 0)
        == lax.broadcasted_iota(jnp.int32, (rank, rank), 1)
    ).astype(jnp.float32)
    total = jnp.sum(jnp.sum(gram * eye, axis=0, keepdims=True), axis=1, keepdims=True)
    scale = jnp.sqrt(total) + scale_epsilon
    gram = gram / scale / scale
    product = None
    for sweep in range(SWEEPS):
        factor = coeff_linear * eye + coeff_square * gram + coeff_fourth * mix(gram, gram)
        product = factor if product is None else mix(product, factor)
        if sweep + 1 < SWEEPS:
            gram = mix(factor, mix(gram, factor))
    return product, scale


def refresh_kernel(groups, count, *refs):
    def take():
        nonlocal refs
        head, refs = refs[:count], refs[count:]
        return head

    own, powers, full, refreshed = take(), take(), take(), take()
    first, half, second, sums = take(), take(), take(), take()
    grams, gram_full = take(), take()
    gram_own, pair_buf, line_buf = take(), take(), take()
    gather = Gather(groups, own, full, refs[:4])
    scatter = Scatter(groups, grams, pair_buf, line_buf, gram_own, refs[4:8])
    gram_gather = Gather(groups, gram_own, gram_full, refs[8:12])
    send, recv = refs[12:]
    layers, _, depth, rank = powers[0].shape
    me = lax.axis_index("tensor")
    side = lax.rem(me, 2)
    near, far = me + 1 - 2 * side, lax.rem(me + 2, 4)
    greet(groups, (near, far))
    tensor_copies = []

    def exchange(stage, m, src, dst, device):
        copy = remote(src, dst, send.at[stage, m], recv.at[stage, m], {"tensor": device})
        copy.start()
        tensor_copies.append(copy)
        return copy

    to_near = [
        exchange(0, m, powers[m].at[:, 1 - side], first[m], near) for m in range(count)
    ]
    units = len(gather.units)
    for u in range(units):
        gather.send(u)
    to_far = []
    for m in range(count):
        to_near[m].wait_recv()
        half[m][...] = powers[m][:, side] + first[m][...]
        to_far.append(exchange(1, m, half[m], second[m], far))
    for u in range(units):
        gather.hop(u, 1)
    for m in range(count):
        to_far[m].wait_recv()
        sums[m][:, side] = half[m][...] + second[m][...]
        exchange(2, m, sums[m].at[:, side], sums[m].at[:, side], near)
    for m in range(count):
        other = sums[m].at[:, 1 - side]
        remote(other, other, send.at[2, m], recv.at[2, m], {"tensor": near}).wait_recv()
    for u, (m, l) in enumerate(scatter.units):
        lower, upper = sums[m][l, 0], sums[m][l, 1]
        gram = lax.dot_general(
            lower, lower, (((0,), (0,)), ((), ())), precision=highest,
            preferred_element_type=jnp.float32,
        ) + lax.dot_general(
            upper, upper, (((0,), (0,)), ((), ())), precision=highest,
            preferred_element_type=jnp.float32,
        )
        grams[m][l] = gram.reshape(grams[m].shape[1:])
        scatter.send(u)
    events = reduce_events(scatter, gram_gather, [2.0] * units, 0.0, 4.0)
    for step in range(2, groups):
        for u in range(units):
            at = (step - 2) * 18.0 + 18.0 * (u + 1) / units
            events.append((at, functools.partial(gather.hop, u, step)))
    play(events)
    for u, (m, l) in enumerate(scatter.units):
        gram_gather.landed(u)
    for m in range(count):

        def one(l, carry, m=m):
            factor, scale = refresh(gram_full[m][l].reshape(rank, rank))
            for part in range(2):
                refreshed[m][l, part] = mix(sums[m][l, part] / scale, factor)
            return carry

        lax.fori_loop(0, layers, one, 0)
    for u in range(units):
        gather.landed(u)
    for copy in tensor_copies:
        copy.wait_send()
    scatter.drain()
    gram_gather.drain()
    gather.drain()


def refresh_call(own, powers, shard, collective):
    groups = shard // 2
    count = len(own)
    layers, rows, _ = own[0].shape
    widths = [o.shape[2] for o in own]
    depth, rank = powers[0].shape[1:]
    powers = [p.reshape(layers, 2, depth // 2, rank) for p in powers]
    units = count * layers
    vmem = pl.BlockSpec(memory_space=pltpu.VMEM)
    outs = [
        jax.ShapeDtypeStruct((layers, groups, 2, rows, w), jnp.float32) for w in widths
    ] + [jax.ShapeDtypeStruct(p.shape, jnp.float32) for p in powers]
    halves = [pltpu.VMEM((layers, depth // 2, rank), jnp.float32)] * count
    sums = [pltpu.VMEM((layers, 2, depth // 2, rank), jnp.float32)] * count
    squares = [pltpu.VMEM((layers, groups, 2, rows, rank), jnp.float32)] * count
    result = pl.pallas_call(
        functools.partial(refresh_kernel, groups, count),
        out_shape=outs,
        in_specs=[vmem] * (2 * count),
        out_specs=[vmem] * len(outs),
        scratch_shapes=halves * 3
        + sums
        + squares * 2
        + reduce_scratch(layers, groups, rows, [rank] * count)
        + gather_sems(units, groups)
        + scatter_sems(units, groups)
        + gather_sems(units, groups)
        + [pltpu.SemaphoreType.DMA((3, count))] * 2,
        compiler_params=pltpu.CompilerParams(
            collective_id=collective, has_side_effects=True, vmem_limit_bytes=VMEM_LIMIT
        ),
        name="gather_refresh",
    )(*own, *powers)
    whole = [r.reshape(layers, rank, r.shape[4]) for r in result[:count]]
    return whole, [r.reshape(layers, depth, rank) for r in result[count:]]


def local(shard, *args):
    gradients, bases, moments_in = args[0:2], args[2:4], args[4:8]
    partial = [
        jnp.einsum("ldr,ldn->lrn", basis, gradient, precision=high)
        for gradient, basis in zip(gradients, bases)
    ]
    flipped = [jnp.transpose(a, (1, 0, 2)) for a in moments_in]
    projected, (moment, variance, direction) = reduce_call(
        partial, flipped[0::2], flipped[1::2], shard, 1
    )
    partial_power = [
        jnp.einsum("ldn,lrn->ldr", gradient, rows, precision=high)
        for gradient, rows in zip(gradients, projected)
    ]
    directions, refreshed = refresh_call(direction, partial_power, shard, 2)
    updates = [
        jnp.einsum("ldr,lrn->ldn", basis, rows, precision=high)
        for basis, rows in zip(bases, directions)
    ]
    back = [jnp.transpose(a, (1, 0, 2)) for pair in zip(moment, variance) for a in pair]
    return (*updates, *back, *refreshed)


def solution(mesh):
    wide, low, basis = P(None, "shard", "tensor"), P("shard", None, "tensor"), P(None, "shard", None)
    return jax.shard_map(
        functools.partial(local, mesh.shape["shard"]),
        mesh=mesh,
        in_specs=(wide, wide, basis, basis, low, low, low, low),
        out_specs=(wide, wide, low, low, low, low, basis, basis),
        check_vma=False,
    )
```

time: 985 us -> 345 us (0.35)
  waiting for transfers between devices: 836 us -> 0 us
  Pallas kernels: 0 us -> 315 us
  matrix products: 80.2 us -> 24.9 us
  blocking collectives: 21.3 us -> 0 us
  between operations: 15.1 us -> 0.74 us
  local copies, waits for them, and re-layouts: 17.4 us -> 4.75 us
    pallas_call x0 -> x2, Pallas kernels: none -> 315 us  [the longest x1 167 us: reduce_call(): pl.pallas_call(functools.partial(reduce_kernel, groups, count), out_shape...]
    unnamed x10 -> x0, waiting for transfers between devices: 301 us -> none
    psum x4 -> x0, waiting for transfers between devices: 292 us -> none  [the longest x3 256 us: orthogonalize(): grams = lax.psum((gram_of(first_current), gram_of(second_current)), 'shard')]
    all_gather x4 -> x0, waiting for transfers between devices: 242 us -> none  [the longest x2 122 us: adapt_matrix(): lax.all_gather(projected, 'shard', axis=0, tiled=True)]
    dot_general x24 -> x6, matrix products: 80.2 us -> 24.9 us  [the longest x2 8.85 us: local(): jnp.einsum('ldr,ldn->lrn', basis, gradient, precision=high)]
    psum x1 -> x0, blocking collectives: 21.3 us -> none  [orthogonalize(): lax.psum((jnp.sum(first_power * first_power, axis=(1, 2)), jnp.sum(second...]
    transpose x2 -> x0, local copies, waits for them, and re-layouts: 11.9 us -> none  [adapt_matrix(): jnp.einsum('ldr,ldn->rln', columns, gradient, precision=highest)]
  transfers between devices with their start and end apart: 9 -> 0, of which waited for: 9 -> 0; matrix products, arithmetic and copies ran while one was open for 3% -> 0% of each run, Pallas kernels for 0% -> 0%
where the time goes in v2:
time: 345 us
  Pallas kernels  315 us (91%)
  matrix products  24.9 us (7%)
  local copies, waits for them, and re-layouts  4.75 us (1%)
    pallas_call x1, Pallas kernels, reduce_call(): pl.pallas_call(functools.partial(reduce_kernel, groups, count), out_shape...  167 us
    pallas_call x1, Pallas kernels, refresh_call(): pl.pallas_call(functools.partial(refresh_kernel, groups, count), out_shap...  147 us
    dot_general x2, matrix products, local(): jnp.einsum('ldr,ldn->lrn', basis, gradient, precision=high)  8.85 us
    dot_general x2, matrix products, local(): jnp.einsum('ldr,lrn->ldn', basis, rows, precision=high)  8.1 us
    dot_general x2, matrix products, local(): jnp.einsum('ldn,lrn->ldr', gradient, rows, precision=high)  7.94 us

profile of v2, /device:TPU:0, one launch (start us, length us, event | category | flops | bytes accessed | tf_op | source)
XLA Modules:
  0.0 345.0 jit_solution(5488418343578463093)
XLA Ops:
  0.6 0.0 copy-start
  0.6 0.0 copy-start.2
  0.7 4.4 %fusion.1 = f32[3,256,768]{2,1,0:T(8,128)} fusion(f32[3,192,256]{2,1,0:T(8,128)} %param.11, f32[3,192,768]{2,1,0:T(8,128)} %param.9), kind=kOutput, calls=%fused_computation.3 | convolution fusion | flops 679477248 | bytes 4718592 | tf_op jit(solution)/shard_map/ldr,ldn->lrn/dot_general | solution.py:439
  5.1 0.0 copy-done
  5.1 4.4 %fusion = f32[3,256,1536]{2,1,0:T(8,128)} fusion(f32[3,192,256]{2,1,0:T(8,128)S(1)} %copy-done.2, f32[3,192,1536]{2,1,0:T(8,128)S(1)} %copy-done), kind=kOutput, calls=%fused_computation.2 | convolution fusion | flops 1358954496 | bytes 8847360 | tf_op jit(solution)/shard_map/ldr,ldn->lrn/dot_general | solution.py:439
  9.5 167.3 %reduce_gather_adam.1 = (f32[3,4,2,32,1536]{4,3,2,1,0:T(8,128)}, f32[3,4,2,32,768]{4,3,2,1,0:T(8,128)}, f32[3,32,1536]{2,1,0:T(8,128)}, f32[3,32,768]{2,1,0:T(8,...) custom-call(f32[3,4,2,32,1536]{4,3,2,1,0:T(8,128)} %bitcast.38, ...), custom_call_target="tpu_custom_call" | custom-call | tf_op jit(solution)/shard_map/reduce_gather_adam/pallas_call | solution.py:276
  176.8 0.0 copy-start.1
  176.8 5.8 %fusion.2 = f32[3,256,192]{1,2,0:T(8,128)} fusion(f32[3,256,1536]{2,1,0:T(8,128)} %bitcast.40, f32[3,192,1536]{2,1,0:T(8,128)S(1)} %copy-done), kind=kOutput, calls=%fused_computation.4 | convolution fusion | flops 1358954496 | bytes 8847360 | tf_op jit(solution)/shard_map/ldn,lrn->ldr/dot_general | solution.py:447
  182.6 0.0 copy-done.4
  182.6 2.2 fusion.3
  184.8 147.3 %gather_refresh.1 = (f32[3,4,2,32,1536]{4,3,2,1,0:T(8,128)}, f32[3,4,2,32,768]{4,3,2,1,0:T(8,128)}, f32[3,2,96,256]{3,2,1,0:T(8,128)}, f32[3,2,96,256]{3,2,1,0:T(8,128)}) custom-call(f32[3,32,1536]{2,1,0:T(8,128)} %get-tuple-element.20.refs_0_, f32[3,32,768]{2,1,0:T(8,128)} %get-tuple-element.21.refs_1_, f32[3,2,96,256]{3,2,1,0:T(8,128)} %bitcast.42, ...), custom_call_target="tpu_custom_call" | custom-call | tf_op jit(solution)/shard_map/gather_refresh/pallas_call | solution.py:414
  332.1 0.0 copy-start.3
  332.1 6.0 %convolution_bitcast_fusion = f32[3,192,1536]{2,1,0:T(8,128)} fusion(f32[3,256,1536]{2,1,0:T(8,128)} %bitcast.41, f32[3,192,256]{2,1,0:T(8,128)S(1)} %copy-done.2), kind=kOutput, calls=%fused_computation | convolution fusion | flops 1358954496 | bytes 8847360 | tf_op jit(solution)/shard_map/ldr,lrn->ldn/dot_general | solution.py:452
  338.1 0.0 copy-done.3
  338.1 2.1 convolution_bitcast_fusion.1
  340.3 0.8 copy.22
  341.1 0.8 copy.23
  341.9 0.0 copy-done.11
  341.9 0.7 copy.24
  342.6 0.0 copy-done.10
  342.6 0.7 copy.25
  343.3 0.0 copy-done.9
  343.4 0.8 copy.26
  344.2 0.8 copy.27
  (14 shorter events, 0.0 us)
Async XLA Ops:
  0.6 4.5 %copy-start = (f32[3,192,1536]{2,1,0:T(8,128)S(1)}, f32[3,192,1536]{2,1,0:T(8,128)}, u32[]{:S(2)}) copy-start(f32[3,192,1536]{2,1,0:T(8,128)} %param.8) | copy-start | bytes 10616836
  0.6 4.4 %copy-start.2 = (f32[3,192,256]{2,1,0:T(8,128)S(1)}, f32[3,192,256]{2,1,0:T(8,128)}, u32[]{:S(2)}) copy-start(f32[3,192,256]{2,1,0:T(8,128)} %param.10) | copy-start | bytes 1769476
  176.8 5.8 %copy-start.1 = (f32[3,192,768]{2,1,0:T(8,128)S(1)}, f32[3,192,768]{2,1,0:T(8,128)}, u32[]{:S(2)}) copy-start(f32[3,192,768]{2,1,0:T(8,128)} %param.9) | copy-start | bytes 5308420
  176.8 5.8 %copy-start.4 = (f32[3,4,2,32,768]{4,3,2,1,0:T(8,128)S(1)}, f32[3,4,2,32,768]{4,3,2,1,0:T(8,128)}, u32[]{:S(2)}) copy-start(f32[3,4,2,32,768]{4,3,2,1,0:T(8,128)} %get-tuple-element.23) | copy-start | bytes 7077892
  332.1 6.0 %copy-start.3 = (f32[3,192,256]{2,1,0:T(8,128)S(1)}, f32[3,192,256]{2,1,0:T(8,128)}, u32[]{:S(2)}) copy-start(f32[3,192,256]{2,1,0:T(8,128)} %param.11) | copy-start | bytes 1769476
  332.1 6.0 %copy-start.5 = (f32[3,4,2,32,768]{4,3,2,1,0:T(8,128)S(1)}, f32[3,4,2,32,768]{4,3,2,1,0:T(8,128)}, u32[]{:S(2)}) copy-start(f32[3,4,2,32,768]{4,3,2,1,0:T(8,128)} %get-tuple-element.25) | copy-start | bytes 7077892
  338.1 2.2 copy-start.7
  338.1 3.0 copy-start.6
  338.1 3.8 %copy-start.11 = (f32[3,32,768]{2,1,0:T(8,128)S(1)}, f32[3,32,768]{2,1,0:T(8,128)}, u32[]{:S(2)}) copy-start(f32[3,32,768]{2,1,0:T(8,128)} %get-tuple-element.28) | copy-start | bytes 884740
  338.1 4.5 %copy-start.10 = (f32[3,32,768]{2,1,0:T(8,128)S(1)}, f32[3,32,768]{2,1,0:T(8,128)}, u32[]{:S(2)}) copy-start(f32[3,32,768]{2,1,0:T(8,128)} %get-tuple-element.29) | copy-start | bytes 884740
  338.1 5.2 %copy-start.9 = (f32[3,2,96,256]{3,2,1,0:T(8,128)S(1)}, f32[3,2,96,256]{3,2,1,0:T(8,128)}, u32[]{:S(2)}) copy-start(f32[3,2,96,256]{3,2,1,0:T(8,128)} %get-tuple-element.30) | copy-start | bytes 1769476
  338.1 6.0 %copy-start.8 = (f32[3,2,96,256]{3,2,1,0:T(8,128)S(1)}, f32[3,2,96,256]{3,2,1,0:T(8,128)}, u32[]{:S(2)}) copy-start(f32[3,2,96,256]{3,2,1,0:T(8,128)} %get-tuple-element.31) | copy-start | bytes 1769476

commit v3 on v2

--- a/solution.py
+++ b/solution.py
@@ -78,47 +78,66 @@
 
 
 class Gather:
-    def __init__(self, groups, own, full, sems):
+    def __init__(self, groups, own, full, sems, early=()):
         self.groups, self.own, self.full, self.sems = groups, own, full, sems
         self.units = units_of(own)
+        self.early = early
         self.started = []
 
+    def to_pair(self, u, step, source, target):
+        _, _, xs, xr = self.sems
+        copy = remote(source, target, xs.at[u, step], xr.at[u, step], pair_of())
+        copy.start()
+        self.started.append(copy)
+
+    def ahead(self, u, step, source, target):
+        zs, zr, _, _ = self.sems
+        copy = remote(source, target, zs.at[u, step], zr.at[u, step], right_of(self.groups))
+        copy.start()
+        self.started.append(copy)
+
     def send(self, u):
         m, l = self.units[u]
         line, side = place()
-        zs, zr, xs, xr = self.sems
         source, target = self.own[m].at[l], self.full[m].at[l, line, side]
-        ahead = remote(source, target, zs.at[u, 1], zr.at[u, 1], right_of(self.groups))
-        ahead.start()
-        pair = remote(source, target, xs.at[u, 0], xr.at[u, 0], pair_of())
-        pair.start()
+        if (m, l) not in self.early:
+            self.ahead(u, 1, source, target)
+        self.to_pair(u, 0, source, target)
         self.full[m][l, line, side] = self.own[m][l]
-        self.started += [ahead, pair]
+
+    def from_pair(self, u, step):
+        m, l = self.units[u]
+        line, side = place()
+        _, _, xs, xr = self.sems
+        source = lax.rem(line + self.groups - step, self.groups)
+        block = self.full[m].at[l, source, 1 - side]
+        remote(block, block, xs.at[u, step], xr.at[u, step], pair_of()).wait_recv()
+
+    def turn(self, u):
+        m, l = self.units[u]
+        if (m, l) in self.early:
+            line, _ = place()
+            self.from_pair(u, 0)
+            block = self.full[m].at[l, line]
+            self.ahead(u, 1, block, block)
 
     def hop(self, u, step):
         m, l = self.units[u]
         line, side = place()
-        zs, zr, xs, xr = self.sems
-        block = self.full[m].at[l, lax.rem(line + self.groups - step, self.groups), side]
+        zs, zr, _, _ = self.sems
+        early = (m, l) in self.early
+        source = lax.rem(line + self.groups - step, self.groups)
+        block = self.full[m].at[l, source] if early else self.full[m].at[l, source, side]
         remote(block, block, zs.at[u, step], zr.at[u, step], right_of(self.groups)).wait_recv()
         if step + 1 < self.groups:
-            ahead = remote(
-                block, block, zs.at[u, step + 1], zr.at[u, step + 1], right_of(self.groups)
-            )
-            ahead.start()
-            self.started.append(ahead)
-        pair = remote(block, block, xs.at[u, step], xr.at[u, step], pair_of())
-        pair.start()
-        self.started.append(pair)
+            self.ahead(u, step + 1, block, block)
+        if not early:
+            self.to_pair(u, step, block, block)
 
     def landed(self, u):
-        m, l = self.units[u]
-        line, side = place()
-        zs, zr, xs, xr = self.sems
-        for step in range(self.groups):
-            source = lax.rem(line + self.groups - step, self.groups)
-            block = self.full[m].at[l, source, 1 - side]
-            remote(block, block, xs.at[u, step], xr.at[u, step], pair_of()).wait_recv()
+        if self.units[u] not in self.early:
+            for step in range(self.groups):
+                self.from_pair(u, step)
 
     def drain(self):
         for copy in self.started:
@@ -203,6 +222,7 @@
             events.append((clock + delay * step, functools.partial(scatter.hop, u, step)))
         ready = clock + delay * (groups - 1)
         events.append((ready, functools.partial(gather.send, u)))
+        events.append((ready + delay * 0.5, functools.partial(gather.turn, u)))
         if finish is not None:
             events.append((ready, functools.partial(finish, u)))
         for step in range(1, groups):
@@ -225,7 +245,7 @@
     full, moments, variances, directions = take(), take(), take(), take()
     own, pair_buf, line_buf = take(), take(), take()
     scatter = Scatter(groups, parts, pair_buf, line_buf, own, refs[:4])
-    gather = Gather(groups, own, full, refs[4:])
+    gather = Gather(groups, own, full, refs[4:], ((count - 1, 0),))
     greet(groups)
     for u in range(len(scatter.units)):
         scatter.send(u)
@@ -294,73 +314,86 @@
     return jnp.dot(left, right, precision=highest, preferred_element_type=jnp.float32)
 
 
-def refresh(gram):
-    rank = gram.shape[-1]
+def refresh(grams):
+    rank = grams[0].shape[-1]
     eye = (
         lax.broadcasted_iota(jnp.int32, (rank, rank), 0)
         == lax.broadcasted_iota(jnp.int32, (rank, rank), 1)
     ).astype(jnp.float32)
-    total = jnp.sum(jnp.sum(gram * eye, axis=0, keepdims=True), axis=1, keepdims=True)
-    scale = jnp.sqrt(total) + scale_epsilon
-    gram = gram / scale / scale
-    product = None
+    totals = [
+        jnp.sum(jnp.sum(g * eye, axis=0, keepdims=True), axis=1, keepdims=True) for g in grams
+    ]
+    scales = [jnp.sqrt(total) + scale_epsilon for total in totals]
+    grams = [g / scale / scale for g, scale in zip(grams, scales)]
+    products = None
     for sweep in range(SWEEPS):
-        factor = coeff_linear * eye + coeff_square * gram + coeff_fourth * mix(gram, gram)
-        product = factor if product is None else mix(product, factor)
+        squared = [mix(g, g) for g in grams]
+        factors = [
+            coeff_linear * eye + coeff_square * g + coeff_fourth * q
+            for g, q in zip(grams, squared)
+        ]
         if sweep + 1 < SWEEPS:
-            gram = mix(factor, mix(gram, factor))
-    return product, scale
+            grams = [mix(g, f) for g, f in zip(grams, factors)]
+            grams = [mix(f, g) for g, f in zip(grams, factors)]
+        if products is None:
+            products = factors
+        else:
+            products = [mix(p, f) for p, f in zip(products, factors)]
+    return products, scales
 
 
 def refresh_kernel(groups, count, *refs):
-    def take():
+    def take(number):
         nonlocal refs
-        head, refs = refs[:count], refs[count:]
+        head, refs = refs[:number], refs[number:]
         return head
 
-    own, powers, full, refreshed = take(), take(), take(), take()
-    first, half, second, sums = take(), take(), take(), take()
-    grams, gram_full = take(), take()
-    gram_own, pair_buf, line_buf = take(), take(), take()
-    gather = Gather(groups, own, full, refs[:4])
+    own, (powers,), full, (refreshed,) = take(count), take(1), take(count), take(1)
+    first, half, second, sums = take(4)
+    grams, gram_full = take(1), take(1)
+    gram_own, pair_buf, line_buf = take(1), take(1), take(1)
+    gather = Gather(groups, own, full, refs[:4], ((count - 1, 0),))
     scatter = Scatter(groups, grams, pair_buf, line_buf, gram_own, refs[4:8])
     gram_gather = Gather(groups, gram_own, gram_full, refs[8:12])
     send, recv = refs[12:]
-    layers, _, depth, rank = powers[0].shape
+    layers, rank = powers.shape[1], powers.shape[4]
     me = lax.axis_index("tensor")
-    side = lax.rem(me, 2)
+    side, mine = lax.rem(me, 2), me // 2
     near, far = me + 1 - 2 * side, lax.rem(me + 2, 4)
     greet(groups, (near, far))
     tensor_copies = []
 
-    def exchange(stage, m, src, dst, device):
-        copy = remote(src, dst, send.at[stage, m], recv.at[stage, m], {"tensor": device})
+    def exchange(stage, src, dst, device):
+        copy = remote(src, dst, send.at[stage], recv.at[stage], {"tensor": device})
         copy.start()
         tensor_copies.append(copy)
         return copy
 
-    to_near = [
-        exchange(0, m, powers[m].at[:, 1 - side], first[m], near) for m in range(count)
-    ]
+    def arrived(stage, block, device):
+        remote(block, block, send.at[stage], recv.at[stage], {"tensor": device}).wait_recv()
+
+    far_near = exchange(0, powers.at[1 - mine, :, 1 - side], first.at[1 - mine], near)
+    own_near = exchange(1, powers.at[mine, :, 1 - side], first.at[mine], near)
     units = len(gather.units)
     for u in range(units):
         gather.send(u)
-    to_far = []
-    for m in range(count):
-        to_near[m].wait_recv()
-        half[m][...] = powers[m][:, side] + first[m][...]
-        to_far.append(exchange(1, m, half[m], second[m], far))
+    far_near.wait_recv()
+    half[1 - mine] = powers[1 - mine, :, side] + first[1 - mine]
+    to_far = exchange(2, half.at[1 - mine], second, far)
+    own_near.wait_recv()
+    half[mine] = powers[mine, :, side] + first[mine]
     for u in range(units):
-        gather.hop(u, 1)
-    for m in range(count):
-        to_far[m].wait_recv()
-        sums[m][:, side] = half[m][...] + second[m][...]
-        exchange(2, m, sums[m].at[:, side], sums[m].at[:, side], near)
-    for m in range(count):
-        other = sums[m].at[:, 1 - side]
-        remote(other, other, send.at[2, m], recv.at[2, m], {"tensor": near}).wait_recv()
-    for u, (m, l) in enumerate(scatter.units):
-        lower, upper = sums[m][l, 0], sums[m][l, 1]
+        gather.turn(u)
+    to_far.wait_recv()
+    low, high_part = half[mine], second[...]
+    sums[:, side] = low + high_part
+    exchange(3, sums.at[:, side], sums.at[:, side], near)
+    for u in range(units):
+        if u < 2:
+            gather.hop(u, 1)
+    arrived(3, sums.at[:, 1 - side], near)
+    for l in range(layers):
+        lower, upper = sums[l, 0], sums[l, 1]
         gram = lax.dot_general(
             lower, lower, (((0,), (0,)), ((), ())), precision=highest,
             preferred_element_type=jnp.float32,
@@ -368,27 +401,30 @@
             upper, upper, (((0,), (0,)), ((), ())), precision=highest,
             preferred_element_type=jnp.float32,
         )
-        grams[m][l] = gram.reshape(grams[m].shape[1:])
-        scatter.send(u)
-    events = reduce_events(scatter, gram_gather, [2.0] * units, 0.0, 4.0)
-    for step in range(2, groups):
+        grams[0][l] = gram.reshape(grams[0].shape[1:])
+        scatter.send(l)
+    events = reduce_events(scatter, gram_gather, [2.0] * layers, 0.0, 3.0)
+    for step in range(1, groups):
         for u in range(units):
-            at = (step - 2) * 18.0 + 18.0 * (u + 1) / units
-            events.append((at, functools.partial(gather.hop, u, step)))
+            if step > 1 or u >= 2:
+                at = (step - 2) * 18.0 + 18.0 * (u + 1) / units
+                events.append((at, functools.partial(gather.hop, u, step)))
     play(events)
-    for u, (m, l) in enumerate(scatter.units):
+    for u in range(layers):
         gram_gather.landed(u)
-    for m in range(count):
-
-        def one(l, carry, m=m):
-            factor, scale = refresh(gram_full[m][l].reshape(rank, rank))
-            for part in range(2):
-                refreshed[m][l, part] = mix(sums[m][l, part] / scale, factor)
-            return carry
-
-        lax.fori_loop(0, layers, one, 0)
+    factors, scales = refresh([gram_full[0][l].reshape(rank, rank) for l in range(layers)])
+    for l in range(layers):
+        refreshed[mine, l, side] = mix(sums[l, side] / scales[l], factors[l])
+    block = refreshed.at[mine, :, side]
+    exchange(4, block, block, far)
+    exchange(5, block, block, near)
+    other = refreshed.at[1 - mine, :, side]
+    arrived(4, other, far)
+    exchange(6, other, other, near)
     for u in range(units):
         gather.landed(u)
+    arrived(5, refreshed.at[mine, :, 1 - side], near)
+    arrived(6, refreshed.at[1 - mine, :, 1 - side], near)
     for copy in tensor_copies:
         copy.wait_send()
     scatter.drain()
@@ -402,35 +438,33 @@
     layers, rows, _ = own[0].shape
     widths = [o.shape[2] for o in own]
     depth, rank = powers[0].shape[1:]
-    powers = [p.reshape(layers, 2, depth // 2, rank) for p in powers]
+    powers = jnp.stack(powers).reshape(count, layers, 2, depth // 2, rank)
     units = count * layers
     vmem = pl.BlockSpec(memory_space=pltpu.VMEM)
     outs = [
         jax.ShapeDtypeStruct((layers, groups, 2, rows, w), jnp.float32) for w in widths
-    ] + [jax.ShapeDtypeStruct(p.shape, jnp.float32) for p in powers]
-    halves = [pltpu.VMEM((layers, depth // 2, rank), jnp.float32)] * count
-    sums = [pltpu.VMEM((layers, 2, depth // 2, rank), jnp.float32)] * count
-    squares = [pltpu.VMEM((layers, groups, 2, rows, rank), jnp.float32)] * count
+    ] + [jax.ShapeDtypeStruct(powers.shape, jnp.float32)]
     result = pl.pallas_call(
         functools.partial(refresh_kernel, groups, count),
         out_shape=outs,
-        in_specs=[vmem] * (2 * count),
+        in_specs=[vmem] * (count + 1),
         out_specs=[vmem] * len(outs),
-        scratch_shapes=halves * 3
-        + sums
-        + squares * 2
-        + reduce_scratch(layers, groups, rows, [rank] * count)
+        scratch_shapes=[pltpu.VMEM((count, layers, depth // 2, rank), jnp.float32)] * 2
+        + [pltpu.VMEM((layers, depth // 2, rank), jnp.float32)]
+        + [pltpu.VMEM((layers, 2, depth // 2, rank), jnp.float32)]
+        + [pltpu.VMEM((layers, groups, 2, rows, rank), jnp.float32)] * 2
+        + reduce_scratch(layers, groups, rows, [rank])
         + gather_sems(units, groups)
-        + scatter_sems(units, groups)
-        + gather_sems(units, groups)
-        + [pltpu.SemaphoreType.DMA((3, count))] * 2,
+        + scatter_sems(layers, groups)
+        + gather_sems(layers, groups)
+        + [pltpu.SemaphoreType.DMA((7,))] * 2,
         compiler_params=pltpu.CompilerParams(
             collective_id=collective, has_side_effects=True, vmem_limit_bytes=VMEM_LIMIT
         ),
         name="gather_refresh",
-    )(*own, *powers)
+    )(*own, powers)
     whole = [r.reshape(layers, rank, r.shape[4]) for r in result[:count]]
-    return whole, [r.reshape(layers, depth, rank) for r in result[count:]]
+    return whole, [r.reshape(layers, depth, rank) for r in result[count]]
 
 
 def local(shard, *args):

time: 345 us -> 332 us (0.962)
  Pallas kernels: 315 us -> 303 us
    pallas_call x1, Pallas kernels: 147 us -> 106 us  [refresh_call(): pl.pallas_call(functools.partial(refresh_kernel, groups, count), out_shap...]
    pallas_call x1, Pallas kernels: 167 us -> 197 us  [reduce_call(): pl.pallas_call(functools.partial(reduce_kernel, groups, count), out_shape...]
where the time goes in v3:
time: 332 us
  Pallas kernels  303 us (91%)
  matrix products  23.3 us (7%)
  local copies, waits for them, and re-layouts  4.32 us (1%)
    pallas_call x1, Pallas kernels, reduce_call(): pl.pallas_call(functools.partial(reduce_kernel, groups, count), out_shape...  197 us
    pallas_call x1, Pallas kernels, refresh_call(): pl.pallas_call(functools.partial(refresh_kernel, groups, count), out_shap...  106 us
    dot_general x2, matrix products, local(): jnp.einsum('ldr,ldn->lrn', basis, gradient, precision=high)  8.85 us
    dot_general x2, matrix products, local(): jnp.einsum('ldr,lrn->ldn', basis, rows, precision=high)  8.1 us

profile of v3, /device:TPU:0, one launch (start us, length us, event | category | flops | bytes accessed | tf_op | source)
XLA Modules:
  0.0 331.9 jit_solution(4055297098458819348)
XLA Ops:
  0.6 0.0 copy-start
  0.6 0.0 copy-start.2
  0.7 4.4 %fusion.2 = f32[3,256,768]{2,1,0:T(8,128)} fusion(f32[3,192,256]{2,1,0:T(8,128)} %param.11, f32[3,192,768]{2,1,0:T(8,128)} %param.9), kind=kOutput, calls=%fused_computation.5 | convolution fusion | flops 679477248 | bytes 4718592 | tf_op jit(solution)/shard_map/ldr,ldn->lrn/dot_general | solution.py:473
  5.1 0.0 copy-done
  5.1 0.0 copy-done.2
  5.1 4.4 %fusion.1 = f32[3,256,1536]{2,1,0:T(8,128)} fusion(f32[3,192,256]{2,1,0:T(8,128)S(1)} %copy-done.2, f32[3,192,1536]{2,1,0:T(8,128)S(1)} %copy-done), kind=kOutput, calls=%fused_computation.4 | convolution fusion | flops 1358954496 | bytes 8847360 | tf_op jit(solution)/shard_map/ldr,ldn->lrn/dot_general | solution.py:473
  9.5 196.7 %reduce_gather_adam.1 = (f32[3,4,2,32,1536]{4,3,2,1,0:T(8,128)}, f32[3,4,2,32,768]{4,3,2,1,0:T(8,128)}, f32[3,32,1536]{2,1,0:T(8,128)}, f32[3,32,768]{2,1,0:T(8,...) custom-call(f32[3,4,2,32,1536]{4,3,2,1,0:T(8,128)} %bitcast.38, ...), custom_call_target="tpu_custom_call" | custom-call | tf_op jit(solution)/shard_map/reduce_gather_adam/pallas_call | solution.py:296
  206.2 0.0 copy-start.1
  206.2 0.0 copy-start.4
  206.2 4.9 %fusion.3 = f32[3,256,192]{1,2,0:T(8,128)S(1)} fusion(f32[3,256,1536]{2,1,0:T(8,128)} %bitcast.40, f32[3,192,1536]{2,1,0:T(8,128)S(1)} %copy-done), kind=kOutput, calls=%fused_computation.6 | convolution fusion | flops 1358954496 | bytes 8847360 | tf_op jit(solution)/shard_map/ldn,lrn->ldr/dot_general | solution.py:481
  211.2 0.0 copy-done.1
  211.2 0.0 copy-done.4
  211.2 1.4 fusion.4
  212.5 1.1 pad_maximum_fusion.refs_2_
  213.6 105.9 %gather_refresh.1 = (f32[3,4,2,32,1536]{4,3,2,1,0:T(8,128)}, f32[3,4,2,32,768]{4,3,2,1,0:T(8,128)}, f32[2,3,2,96,256]{4,3,2,1,0:T(8,128)}) custom-call(f32[3,32,1536]{2,1,0:T(8,128)} %get-tuple-element.19.refs_0_, f32[3,32,768]{2,1,0:T(8,128)} %get-tuple-element.20.refs_1_, f32[2,3,2,96,256]{4,3,2,1,0:T(8,128)} %pad_maximum_fusion.refs_2_), custom_call_target="tpu_custom_call" | custom-call | tf_op jit(solution)/shard_map/gather_refresh/pallas_call | solution.py:447
  319.5 0.0 copy-start.3
  319.5 6.0 %convolution_bitcast_fusion = f32[3,192,1536]{2,1,0:T(8,128)} fusion(f32[3,256,1536]{2,1,0:T(8,128)} %bitcast.41, f32[3,192,256]{2,1,0:T(8,128)S(1)} %copy-done.2), kind=kOutput, calls=%fused_computation | convolution fusion | flops 1358954496 | bytes 8847360 | tf_op jit(solution)/shard_map/ldr,lrn->ldn/dot_general | solution.py:486
  325.5 2.1 convolution_bitcast_fusion.1
  327.7 1.1 fusion
  328.8 0.1 copy-done.8
  328.9 0.8 copy.20
  329.7 0.8 copy.21
  330.5 0.7 copy.22
  331.2 0.7 copy.23
  (12 shorter events, 0.0 us)
Async XLA Ops:
  0.6 4.5 %copy-start = (f32[3,192,1536]{2,1,0:T(8,128)S(1)}, f32[3,192,1536]{2,1,0:T(8,128)}, u32[]{:S(2)}) copy-start(f32[3,192,1536]{2,1,0:T(8,128)} %param.8) | copy-start | bytes 10616836
  0.6 4.4 %copy-start.2 = (f32[3,192,256]{2,1,0:T(8,128)S(1)}, f32[3,192,256]{2,1,0:T(8,128)}, u32[]{:S(2)}) copy-start(f32[3,192,256]{2,1,0:T(8,128)} %param.10) | copy-start | bytes 1769476
  206.2 5.0 %copy-start.1 = (f32[3,192,768]{2,1,0:T(8,128)S(1)}, f32[3,192,768]{2,1,0:T(8,128)}, u32[]{:S(2)}) copy-start(f32[3,192,768]{2,1,0:T(8,128)} %param.9) | copy-start | bytes 5308420
  206.2 5.0 %copy-start.4 = (f32[3,4,2,32,768]{4,3,2,1,0:T(8,128)S(1)}, f32[3,4,2,32,768]{4,3,2,1,0:T(8,128)}, u32[]{:S(2)}) copy-start(f32[3,4,2,32,768]{4,3,2,1,0:T(8,128)} %get-tuple-element.22) | copy-start | bytes 7077892
  319.5 6.0 %copy-start.3 = (f32[3,192,256]{2,1,0:T(8,128)S(1)}, f32[3,192,256]{2,1,0:T(8,128)}, u32[]{:S(2)}) copy-start(f32[3,192,256]{2,1,0:T(8,128)} %param.11) | copy-start | bytes 1769476
  319.5 6.0 %copy-start.5 = (f32[3,4,2,32,768]{4,3,2,1,0:T(8,128)S(1)}, f32[3,4,2,32,768]{4,3,2,1,0:T(8,128)}, u32[]{:S(2)}) copy-start(f32[3,4,2,32,768]{4,3,2,1,0:T(8,128)} %get-tuple-element.24) | copy-start | bytes 7077892
  325.5 2.1 copy-start.6
  327.6 1.2 copy-start.8
  327.6 2.0 copy-start.7
  327.7 2.9 copy-start.10
  327.7 3.6 %copy-start.9 = (f32[3,32,768]{2,1,0:T(8,128)S(1)}, f32[3,32,768]{2,1,0:T(8,128)}, u32[]{:S(2)}) copy-start(f32[3,32,768]{2,1,0:T(8,128)} %get-tuple-element.28) | copy-start | bytes 884740

commit v4 on v3

--- a/solution.py
+++ b/solution.py
@@ -245,7 +245,7 @@
     full, moments, variances, directions = take(), take(), take(), take()
     own, pair_buf, line_buf = take(), take(), take()
     scatter = Scatter(groups, parts, pair_buf, line_buf, own, refs[:4])
-    gather = Gather(groups, own, full, refs[4:], ((count - 1, 0),))
+    gather = Gather(groups, own, full, refs[4:])
     greet(groups)
     for u in range(len(scatter.units)):
         scatter.send(u)

time: 332 us -> 304 us (0.916)
  Pallas kernels: 303 us -> 274 us
    pallas_call x1, Pallas kernels: 197 us -> 167 us  [reduce_call(): pl.pallas_call(functools.partial(reduce_kernel, groups, count), out_shape...]
where the time goes in v4:
time: 304 us
  Pallas kernels  274 us (90%)
  matrix products  23.3 us (8%)
  local copies, waits for them, and re-layouts  4.32 us (1%)
    pallas_call x1, Pallas kernels, reduce_call(): pl.pallas_call(functools.partial(reduce_kernel, groups, count), out_shape...  167 us
    pallas_call x1, Pallas kernels, refresh_call(): pl.pallas_call(functools.partial(refresh_kernel, groups, count), out_shap...  107 us
    dot_general x2, matrix products, local(): jnp.einsum('ldr,ldn->lrn', basis, gradient, precision=high)  8.85 us
    dot_general x2, matrix products, local(): jnp.einsum('ldr,lrn->ldn', basis, rows, precision=high)  8.1 us
    dot_general x2, matrix products, local(): jnp.einsum('ldn,lrn->ldr', gradient, rows, precision=high)  6.31 us

profile of v4, /device:TPU:0, one launch (start us, length us, event | category | flops | bytes accessed | tf_op | source)
XLA Modules:
  0.0 303.7 jit_solution(8646145845886393325)
XLA Ops:
  0.6 0.0 copy-start
  0.6 0.0 copy-start.2
  0.7 4.4 %fusion.2 = f32[3,256,768]{2,1,0:T(8,128)} fusion(f32[3,192,256]{2,1,0:T(8,128)} %param.11, f32[3,192,768]{2,1,0:T(8,128)} %param.9), kind=kOutput, calls=%fused_computation.5 | convolution fusion | flops 679477248 | bytes 4718592 | tf_op jit(solution)/shard_map/ldr,ldn->lrn/dot_general | solution.py:473
  5.1 0.0 copy-done
  5.1 4.4 %fusion.1 = f32[3,256,1536]{2,1,0:T(8,128)} fusion(f32[3,192,256]{2,1,0:T(8,128)S(1)} %copy-done.2, f32[3,192,1536]{2,1,0:T(8,128)S(1)} %copy-done), kind=kOutput, calls=%fused_computation.4 | convolution fusion | flops 1358954496 | bytes 8847360 | tf_op jit(solution)/shard_map/ldr,ldn->lrn/dot_general | solution.py:473
  9.5 167.3 %reduce_gather_adam.1 = (f32[3,4,2,32,1536]{4,3,2,1,0:T(8,128)}, f32[3,4,2,32,768]{4,3,2,1,0:T(8,128)}, f32[3,32,1536]{2,1,0:T(8,128)}, f32[3,32,768]{2,1,0:T(8,...) custom-call(f32[3,4,2,32,1536]{4,3,2,1,0:T(8,128)} %bitcast.38, ...), custom_call_target="tpu_custom_call" | custom-call | tf_op jit(solution)/shard_map/reduce_gather_adam/pallas_call | solution.py:296
  176.8 0.0 copy-start.1
  176.8 0.0 copy-start.4
  176.8 4.9 %fusion.3 = f32[3,256,192]{1,2,0:T(8,128)S(1)} fusion(f32[3,256,1536]{2,1,0:T(8,128)} %bitcast.40, f32[3,192,1536]{2,1,0:T(8,128)S(1)} %copy-done), kind=kOutput, calls=%fused_computation.6 | convolution fusion | flops 1358954496 | bytes 8847360 | tf_op jit(solution)/shard_map/ldn,lrn->ldr/dot_general | solution.py:481
  181.8 1.4 fusion.4
  183.1 1.1 pad_maximum_fusion.refs_2_
  184.2 107.0 %gather_refresh.1 = (f32[3,4,2,32,1536]{4,3,2,1,0:T(8,128)}, f32[3,4,2,32,768]{4,3,2,1,0:T(8,128)}, f32[2,3,2,96,256]{4,3,2,1,0:T(8,128)}) custom-call(f32[3,32,1536]{2,1,0:T(8,128)} %get-tuple-element.19.refs_0_, f32[3,32,768]{2,1,0:T(8,128)} %get-tuple-element.20.refs_1_, f32[2,3,2,96,256]{4,3,2,1,0:T(8,128)} %pad_maximum_fusion.refs_2_), custom_call_target="tpu_custom_call" | custom-call | tf_op jit(solution)/shard_map/gather_refresh/pallas_call | solution.py:447
  291.3 0.0 copy-start.3
  291.3 6.0 %convolution_bitcast_fusion = f32[3,192,1536]{2,1,0:T(8,128)} fusion(f32[3,256,1536]{2,1,0:T(8,128)} %bitcast.41, f32[3,192,256]{2,1,0:T(8,128)S(1)} %copy-done.2), kind=kOutput, calls=%fused_computation | convolution fusion | flops 1358954496 | bytes 8847360 | tf_op jit(solution)/shard_map/ldr,lrn->ldn/dot_general | solution.py:486
  297.3 2.1 convolution_bitcast_fusion.1
  299.4 0.0 copy-start.9
  299.4 1.1 fusion
  300.5 0.1 copy-done.8
  300.7 0.8 copy.20
  301.5 0.8 copy.21
  302.3 0.0 copy-done.10
  302.3 0.7 copy.22
  303.0 0.0 copy-done.9
  303.0 0.7 copy.23
  (12 shorter events, 0.0 us)
Async XLA Ops:
  0.6 4.5 %copy-start = (f32[3,192,1536]{2,1,0:T(8,128)S(1)}, f32[3,192,1536]{2,1,0:T(8,128)}, u32[]{:S(2)}) copy-start(f32[3,192,1536]{2,1,0:T(8,128)} %param.8) | copy-start | bytes 10616836
  0.6 4.4 %copy-start.2 = (f32[3,192,256]{2,1,0:T(8,128)S(1)}, f32[3,192,256]{2,1,0:T(8,128)}, u32[]{:S(2)}) copy-start(f32[3,192,256]{2,1,0:T(8,128)} %param.10) | copy-start | bytes 1769476
  176.8 5.0 %copy-start.1 = (f32[3,192,768]{2,1,0:T(8,128)S(1)}, f32[3,192,768]{2,1,0:T(8,128)}, u32[]{:S(2)}) copy-start(f32[3,192,768]{2,1,0:T(8,128)} %param.9) | copy-start | bytes 5308420
  176.8 5.0 %copy-start.4 = (f32[3,4,2,32,768]{4,3,2,1,0:T(8,128)S(1)}, f32[3,4,2,32,768]{4,3,2,1,0:T(8,128)}, u32[]{:S(2)}) copy-start(f32[3,4,2,32,768]{4,3,2,1,0:T(8,128)} %get-tuple-element.22) | copy-start | bytes 7077892
  291.3 6.0 %copy-start.3 = (f32[3,192,256]{2,1,0:T(8,128)S(1)}, f32[3,192,256]{2,1,0:T(8,128)}, u32[]{:S(2)}) copy-start(f32[3,192,256]{2,1,0:T(8,128)} %param.11) | copy-start | bytes 1769476
  291.3 6.0 %copy-start.5 = (f32[3,4,2,32,768]{4,3,2,1,0:T(8,128)S(1)}, f32[3,4,2,32,768]{4,3,2,1,0:T(8,128)}, u32[]{:S(2)}) copy-start(f32[3,4,2,32,768]{4,3,2,1,0:T(8,128)} %get-tuple-element.24) | copy-start | bytes 7077892
  297.3 2.1 copy-start.6
  299.4 1.2 copy-start.8
  299.4 2.0 copy-start.7
  299.4 2.9 copy-start.10
  299.4 3.6 %copy-start.9 = (f32[3,32,768]{2,1,0:T(8,128)S(1)}, f32[3,32,768]{2,1,0:T(8,128)}, u32[]{:S(2)}) copy-start(f32[3,32,768]{2,1,0:T(8,128)} %get-tuple-element.28) | copy-start | bytes 884740
